TPU v7x, 768 devices: a whole 4x8x12 slice. The times are simulated.
768 devices in a mesh: seq: 24 (over y, z_hi), mp: 32 (over z_lo, x, core).
Axes of the slice: x: 4, y: 8, z: 12 (z_hi: 3, z_lo: 4; z = z_hi * 4 + z_lo), core: 2. Of those that a mesh axis runs over, the one named last changes fastest.
Arguments:
- tokens: bfloat16 [3072, 4096], P('seq', 'mp'), may hold values from -68 to 68
- w_qkv: bfloat16 [3, 4096, 4096], P(None, None, 'mp'), may hold values from -0.09375 to 0.09375
- w_pos: bfloat16 [4096, 4096], P(None, 'mp'), may hold values from -0.09375 to 0.09375
- w_out: bfloat16 [4096, 4096], P('mp'), may hold values from -0.09375 to 0.09375
- content_bias: float32 [32, 128], P('mp'), may hold values from -4 to 4
- position_bias: float32 [32, 128], P('mp'), may hold values from -4 to 4
- doc_ids: int32 [3072], P('seq'), may hold values from 0 to 23, never falling along the last dimension, each value on 1 to 256 neighbouring positions
Outputs:
- attn_out: bfloat16 [3072, 4096], P('seq', 'mp')
All inputs are finite; a program needn't handle non-finite values.
Results may differ from a plain program's by a relative error of at most 0.0067.
Values may be sent and summed in bfloat16 or wider, within the bound.
A program may use at most 32 MiB of HBM per device.

v0:
```python
import jax
import jax.numpy as jnp
import numpy as np
from jax import lax
from jax.experimental import pallas as pl
from jax.experimental.pallas import tpu as pltpu
from jax.sharding import PartitionSpec as P

MESH = pl.DeviceIdType.MESH
F32 = jnp.float32
BF16 = jnp.bfloat16


def sinus_reversed(count, width):
    place = np.arange(count, dtype=np.float32)[::-1, None]
    freqs = np.float32(1.0) / np.power(
        np.float32(10000.0), np.arange(0, width, 2, dtype=np.float32) / np.float32(width)
    )
    angle = place * freqs[None, :].astype(np.float32)
    table = np.concatenate([np.sin(angle), np.cos(angle)], axis=1)
    return table.astype(jnp.bfloat16)


def dot(a, b):
    return jnp.dot(a, b, preferred_element_type=F32)


def dot_t(a, b):
    return lax.dot_general(a, b, (((1,), (1,)), ((), ())), preferred_element_type=F32)


def kernel(
    tok_in, wqkv, wpos, wout, cbias_in, pbias_in, doc_in, sinus, out,
    cbias, pbias, doc, toks, wv, wp, sn, wo, acc, kvs, kvm, docm, ho, part, rcv,
    lsem, tok_ss, tok_rs, w_ss, w_rs, kv_ss, kv_rs, ho_ss, ho_rs, p_ss, p_rs,
):
    seq = lax.axis_index("seq")
    me = lax.axis_index("mp")
    n_seq = lax.axis_size("seq")
    z, x, c = me // 8, (me // 2) % 4, me % 2
    xc = me % 8
    nxt, prv = (seq + 1) % n_seq, (seq + n_seq - 1) % n_seq
    xr, xl = (x + 1) % 4, (x + 3) % 4
    dirn = 1 - 2 * c
    x_up, x_dn = (x - dirn + 4) % 4, (x + dirn + 4) % 4
    x_far = (x + 2) % 4
    inner = (z // 2 + z % 2) % 2
    za, zb, zc = z + 1 - 2 * (z % 2), 3 - z, (z + 2) % 4
    zo = [z, za, inner * zb + (1 - inner) * zc, inner * zc + (1 - inner) * zb]

    def mp_of(zz, xx, cc):
        return (zz * 4 + xx) * 2 + cc

    barrier = pltpu.get_barrier_semaphore()
    for k in range(1, 8):
        pl.semaphore_signal(
            barrier, inc=1, device_id={"mp": z * 8 + (xc + k) % 8}, device_id_type=MESH
        )
    for k in range(1, 4):
        pl.semaphore_signal(
            barrier, inc=1, device_id={"mp": mp_of(zo[k], x, c)}, device_id_type=MESH
        )
    pl.semaphore_signal(barrier, inc=1, device_id={"seq": prv}, device_id_type=MESH)

    ld_tok = pltpu.make_async_copy(tok_in, toks.at[me], lsem.at[4])
    ld_tok.start()
    ld_doc = pltpu.make_async_copy(doc_in, doc, lsem.at[5])
    ld_doc.start()
    ld_cb = pltpu.make_async_copy(cbias_in, cbias, lsem.at[6])
    ld_cb.start()
    ld_pb = pltpu.make_async_copy(pbias_in, pbias, lsem.at[7])
    ld_pb.start()
    ld_sn = pltpu.make_async_copy(sinus, sn, lsem.at[0])
    ld_wp = pltpu.make_async_copy(wpos, wp, lsem.at[1])
    ld_wv = pltpu.make_async_copy(wqkv, wv, lsem.at[2])
    ld_sn.start()
    ld_wp.start()
    ld_wv.start()
    tok = toks.at[me]
    ld_tok.wait()
    ld_doc.wait()

    pl.semaphore_wait(barrier, 11)

    sends = []

    def push(src, slot, target):
        n = len(sends)
        copy = pltpu.make_async_remote_copy(
            src_ref=src,
            dst_ref=toks.at[slot],
            send_sem=tok_ss.at[n],
            recv_sem=tok_rs.at[slot],
            device_id={"mp": target},
            device_id_type=MESH,
        )
        copy.start()
        sends.append(copy)

    def landed(slot):
        pltpu.make_async_remote_copy(
            src_ref=tok,
            dst_ref=toks.at[slot],
            send_sem=tok_ss.at[0],
            recv_sem=tok_rs.at[slot],
            device_id={"mp": me},
            device_id_type=MESH,
        ).wait_recv()

    push(tok, me, mp_of(zo[1], x, c))
    push(tok, me, mp_of(z, xr, c))
    push(tok, me, mp_of(z, xl, c))
    push(tok, me, mp_of(zo[2], x, c))
    push(tok, me, mp_of(zo[3], x, c))
    push(tok, me, mp_of(z, x, 1 - c))
    doc_copy = pltpu.make_async_remote_copy(
        src_ref=doc,
        dst_ref=docm,
        send_sem=kv_ss.at[2],
        recv_sem=kv_rs.at[2],
        device_id={"seq": nxt},
        device_id_type=MESH,
    )
    doc_copy.start()

    ld_sn.wait()
    ld_wp.wait()
    rel = dot(sn[...], wp[...]).astype(BF16)

    def from_z(k):
        slot = mp_of(zo[k], x, c)
        landed(slot)
        push(toks.at[slot], slot, mp_of(z, xr, c))
        push(toks.at[slot], slot, mp_of(z, xl, c))
        if k == 3:
            push(toks.at[slot], slot, mp_of(z, x_far, c))
        push(toks.at[slot], slot, mp_of(z, x, 1 - c))

    def from_x(k):
        slot = mp_of(zo[k], x_up, c)
        landed(slot)
        if k < 3:
            push(toks.at[slot], slot, mp_of(z, x_dn, c))
        push(toks.at[slot], slot, mp_of(z, x, 1 - c))
        slot = mp_of(zo[k], x_dn, c)
        landed(slot)
        push(toks.at[slot], slot, mp_of(z, x, 1 - c))

    def from_far(k):
        slot = mp_of(zo[k], x_far, c)
        landed(slot)
        push(toks.at[slot], slot, mp_of(z, x, 1 - c))

    def from_core(k):
        for xx in (x, x_up, x_dn, x_far):
            landed(mp_of(zo[k], xx, 1 - c))

    def project(k):
        zz = zo[k]
        left = jnp.concatenate([toks[zz * 8 + j] for j in range(8)], axis=1)
        rows = pl.ds(pl.multiple_of(zz * 1024, 1024), 1024)
        right = jnp.concatenate([wv[0, rows, :], wv[1, rows, :], wv[2, rows, :]], axis=1)
        term = dot(left, right)
        if k == 0:
            acc[...] = term
        else:
            acc[...] += term

    for k in (1, 2, 3):
        from_z(k)
    for k in (0, 1, 2, 3):
        from_x(k)
    for k in (0, 1, 2, 3):
        from_far(k)

    w_copies = []
    for k in (1, 7, 2, 6, 3, 5, 4):
        to = (xc + k) % 8
        for zz in range(4):
            cols = pl.ds(pl.multiple_of((zz * 8 + to) * 128, 128), 128)
            pltpu.make_async_remote_copy(
                src_ref=wout.at[:, cols],
                dst_ref=wo.at[xc, zz],
                send_sem=w_ss.at[k],
                recv_sem=w_rs.at[xc],
                device_id={"mp": z * 8 + to},
                device_id_type=MESH,
            ).start()
    for zz in range(4):
        cols = pl.ds(pl.multiple_of((zz * 8 + xc) * 128, 128), 128)
        pltpu.make_async_copy(wout.at[:, cols], wo.at[xc, zz], lsem.at[3]).start()

    ld_wv.wait()
    for k in (0, 1, 2, 3):
        from_core(k)
        project(k)

    kvs[0] = acc[:, 128:256].astype(BF16)
    kvs[1] = acc[:, 256:384].astype(BF16)
    kv_copies = []
    for i in range(2):
        copy = pltpu.make_async_remote_copy(
            src_ref=kvs.at[i],
            dst_ref=kvm.at[i],
            send_sem=kv_ss.at[i],
            recv_sem=kv_rs.at[i],
            device_id={"seq": nxt},
            device_id_type=MESH,
        )
        copy.start()
        kv_copies.append(copy)

    ld_cb.wait()
    ld_pb.wait()
    query = acc[:, 0:128]
    qc = (query + cbias[...]).astype(BF16)
    qp = (query + pbias[...]).astype(BF16)
    pos = pltpu.roll(dot_t(qp, rel), 129, 1, stride=1, stride_axis=0)
    scale = F32(1.0) / jnp.sqrt(F32(128.0))
    own_doc = doc[...]
    row_doc = jnp.transpose(jnp.broadcast_to(own_doc, (128, 128)))
    rows = lax.broadcasted_iota(jnp.int32, (128, 128), 0)
    cols = lax.broadcasted_iota(jnp.int32, (128, 128), 1)
    ok_own = (cols <= rows) & (row_doc == own_doc)
    s_own = (dot_t(qc, kvs[0]) + pos[:, 128:256]) * scale
    s_own = jnp.where(ok_own, s_own, F32(-1e30))
    top_own = jnp.max(s_own, axis=1, keepdims=True)

    doc_copy.wait_recv()
    ok_mem = (row_doc == docm[...]) & (seq > 0)
    kv_copies[0].wait_recv()
    s_mem = (dot_t(qc, kvm[0]) + pos[:, 0:128]) * scale
    s_mem = jnp.where(ok_mem, s_mem, F32(-1e30))
    top = jnp.maximum(top_own, jnp.max(s_mem, axis=1, keepdims=True))
    e_own = jnp.where(ok_own, jnp.exp(s_own - top), F32(0.0))
    e_mem = jnp.where(ok_mem, jnp.exp(s_mem - top), F32(0.0))
    total = jnp.sum(e_own, axis=1, keepdims=True) + jnp.sum(e_mem, axis=1, keepdims=True)
    w_own = (e_own / total).astype(BF16)
    w_mem = (e_mem / total).astype(BF16)
    kv_copies[1].wait_recv()
    head = dot(w_own, kvs[1]) + dot(w_mem, kvm[1])
    ho[xc] = head.astype(BF16)

    ho_copies = []
    for k in (1, 7, 2, 6, 3, 5, 4):
        copy = pltpu.make_async_remote_copy(
            src_ref=ho.at[xc],
            dst_ref=ho.at[xc],
            send_sem=ho_ss.at[k],
            recv_sem=ho_rs.at[xc],
            device_id={"mp": z * 8 + (xc + k) % 8},
            device_id_type=MESH,
        )
        copy.start()
        ho_copies.append(copy)

    for k in range(1, 8):
        slot = (xc + k) % 8
        pltpu.make_async_remote_copy(
            src_ref=wo.at[slot],
            dst_ref=wo.at[slot],
            send_sem=w_ss.at[0],
            recv_sem=w_rs.at[slot],
            device_id={"mp": me},
            device_id_type=MESH,
        ).wait_recv()
    pltpu.make_async_copy(wo.at[xc], wo.at[xc], lsem.at[3]).wait()
    for k in range(1, 8):
        slot = (xc + k) % 8
        pltpu.make_async_remote_copy(
            src_ref=ho.at[slot],
            dst_ref=ho.at[slot],
            send_sem=ho_ss.at[0],
            recv_sem=ho_rs.at[slot],
            device_id={"mp": me},
            device_id_type=MESH,
        ).wait_recv()

    heads = jnp.concatenate([ho[j] for j in range(8)], axis=1)
    p_copies = []
    for k in (3, 2, 1, 0):
        zz = zo[k]
        right = jnp.concatenate([wo[j, zz] for j in range(8)], axis=0)
        part[zz] = dot(heads, right)
        if k > 0:
            copy = pltpu.make_async_remote_copy(
                src_ref=part.at[zz],
                dst_ref=rcv.at[z],
                send_sem=p_ss.at[k],
                recv_sem=p_rs.at[z],
                device_id={"mp": mp_of(zz, x, c)},
                device_id_type=MESH,
            )
            copy.start()
            p_copies.append(copy)
    result = part[z]
    for k in (1, 2, 3):
        zz = zo[k]
        pltpu.make_async_remote_copy(
            src_ref=rcv.at[zz],
            dst_ref=rcv.at[zz],
            send_sem=p_ss.at[0],
            recv_sem=p_rs.at[zz],
            device_id={"mp": me},
            device_id_type=MESH,
        ).wait_recv()
        result = result + rcv[zz]
    out[...] = result.astype(BF16)

    for copy in sends:
        copy.wait_send()
    for k in range(1, 8):
        pltpu.make_async_remote_copy(
            src_ref=wo.at[xc],
            dst_ref=wo.at[xc],
            send_sem=w_ss.at[k],
            recv_sem=w_rs.at[xc],
            device_id={"mp": me},
            device_id_type=MESH,
        ).wait_send()
    for copy in kv_copies + [doc_copy] + ho_copies + p_copies:
        copy.wait_send()


def shards(tokens, w_qkv, w_pos, w_out, content_bias, position_bias, doc_ids):
    vmem = pl.BlockSpec(memory_space=pltpu.VMEM)
    hbm = pl.BlockSpec(memory_space=pltpu.HBM)
    sinus = jnp.asarray(sinus_reversed(256, 4096))
    operands = (
        tokens, w_qkv, w_pos, w_out, content_bias, position_bias, doc_ids.reshape(1, 128), sinus
    )
    operands = [pltpu.with_memory_space_constraint(a, pltpu.HBM) for a in operands]
    return pl.pallas_call(
        kernel,
        out_shape=pltpu.VMEM((128, 128), BF16),
        in_specs=[hbm] * 8,
        out_specs=vmem,
        scratch_shapes=[
            pltpu.VMEM((1, 128), F32),
            pltpu.VMEM((1, 128), F32),
            pltpu.VMEM((1, 128), jnp.int32),
            pltpu.VMEM((32, 128, 128), BF16),
            pltpu.VMEM((3, 4096, 128), BF16),
            pltpu.VMEM((4096, 128), BF16),
            pltpu.VMEM((256, 4096), BF16),
            pltpu.VMEM((8, 4, 128, 128), BF16),
            pltpu.VMEM((128, 384), F32),
            pltpu.VMEM((2, 128, 128), BF16),
            pltpu.VMEM((2, 128, 128), BF16),
            pltpu.VMEM((1, 128), jnp.int32),
            pltpu.VMEM((8, 128, 128), BF16),
            pltpu.VMEM((4, 128, 128), F32),
            pltpu.VMEM((4, 128, 128), F32),
            pltpu.SemaphoreType.DMA((8,)),
            pltpu.SemaphoreType.DMA((31,)),
            pltpu.SemaphoreType.DMA((32,)),
            pltpu.SemaphoreType.DMA((8,)),
            pltpu.SemaphoreType.DMA((8,)),
            pltpu.SemaphoreType.DMA((3,)),
            pltpu.SemaphoreType.DMA((3,)),
            pltpu.SemaphoreType.DMA((8,)),
            pltpu.SemaphoreType.DMA((8,)),
            pltpu.SemaphoreType.DMA((4,)),
            pltpu.SemaphoreType.DMA((4,)),
        ],
        compiler_params=pltpu.CompilerParams(
            collective_id=0, has_side_effects=True, vmem_limit_bytes=20 * 1024 * 1024
        ),
        name="layer",
    )(*operands)


def solution(mesh):
    in_specs = (
        P("seq", "mp"),
        P(None, None, "mp"),
        P(None, "mp"),
        P("mp", None),
        P("mp", None),
        P("mp", None),
        P("seq"),
    )
    out_specs = P("seq", "mp")
    return jax.shard_map(shards, mesh=mesh, in_specs=in_specs, out_specs=out_specs, check_vma=False)
```

profile of v0, /device:TPU:6, one launch (start us, length us, event | category | flops | bytes accessed | tf_op | source)
XLA Modules:
  0.0 50.9 jit_solution(13385615149540709836)
XLA Ops:
  0.0 50.3 %layer.1 = bf16[128,128]{1,0:T(8,128)(2,1)S(1)} custom-call(bf16[128,128]{1,0:T(8,128)(2,1)} %tok_in.1, bf16[3,4096,128]{2,1,0:T(8,128)(2,1)} %wqkv.1, bf16[4096,128]{1,0:T(8,128)(2,1)} %wpos.1, bf16[128,4096]{1,0:T(8,128)(2,1)} %wout.1, f32[1,128]{1,0:T(1,128)} %cbias_in.1, f32[1,128]{1,0:T(1,128)} %pbias_in.1, s32[1,128]{1,0:T(1,128)} %bitcast.1, ...), custom_call_target="tpu_custom_call" | custom-call | tf_op jit(solution)/shard_map/layer/pallas_call | solution.py:333
  50.3 0.6 %copy.10 = bf16[128,128]{1,0:T(8,128)(2,1)} copy(bf16[128,128]{1,0:T(8,128)(2,1)S(1)} %layer.1) | data formatting | bytes 65536
where the time goes:
time: 51.1 us; the launch traced here: 50.9 us
  Pallas kernels  50.3 us (98%)
  local copies, waits for them, and re-layouts  0.62 us (1%)
    pallas_call x1, Pallas kernels, shards(): pl.pallas_call(kernel, out_shape=pltpu.VMEM((128, 128), BF16), in_specs=[...  50.3 us

commit v1 on v0

--- a/solution.py
+++ b/solution.py
@@ -32,7 +32,7 @@
 def kernel(
     tok_in, wqkv, wpos, wout, cbias_in, pbias_in, doc_in, sinus, out,
     cbias, pbias, doc, toks, wv, wp, sn, wo, acc, kvs, kvm, docm, ho, part, rcv,
-    lsem, tok_ss, tok_rs, w_ss, w_rs, kv_ss, kv_rs, ho_ss, ho_rs, p_ss, p_rs,
+    via, via_ss, via_rs, lsem, tok_ss, tok_rs, w_ss, w_rs, kv_ss, kv_rs, ho_ss, ho_rs, p_ss, p_rs,
 ):
     seq = lax.axis_index("seq")
     me = lax.axis_index("mp")
@@ -40,6 +40,7 @@
     z, x, c = me // 8, (me // 2) % 4, me % 2
     xc = me % 8
     nxt, prv = (seq + 1) % n_seq, (seq + n_seq - 1) % n_seq
+    has_next, has_prev = seq < n_seq - 1, seq > 0
     xr, xl = (x + 1) % 4, (x + 3) % 4
     dirn = 1 - 2 * c
     x_up, x_dn = (x - dirn + 4) % 4, (x + dirn + 4) % 4
@@ -60,7 +61,9 @@
         pl.semaphore_signal(
             barrier, inc=1, device_id={"mp": mp_of(zo[k], x, c)}, device_id_type=MESH
         )
-    pl.semaphore_signal(barrier, inc=1, device_id={"seq": prv}, device_id_type=MESH)
+    @pl.when(has_prev)
+    def _():
+        pl.semaphore_signal(barrier, inc=1, device_id={"seq": prv}, device_id_type=MESH)
 
     ld_tok = pltpu.make_async_copy(tok_in, toks.at[me], lsem.at[4])
     ld_tok.start()
@@ -77,10 +80,12 @@
     ld_wp.start()
     ld_wv.start()
     tok = toks.at[me]
-    ld_tok.wait()
-    ld_doc.wait()
-
-    pl.semaphore_wait(barrier, 11)
+    with jax.named_scope("m_tok"):
+        ld_tok.wait()
+        ld_doc.wait()
+
+    with jax.named_scope("m_bar"):
+        pl.semaphore_wait(barrier, 10 + has_next.astype(jnp.int32))
 
     sends = []
 
@@ -121,25 +126,81 @@
         device_id={"seq": nxt},
         device_id_type=MESH,
     )
-    doc_copy.start()
-
-    ld_sn.wait()
-    ld_wp.wait()
-    rel = dot(sn[...], wp[...]).astype(BF16)
+
+    @pl.when(has_next)
+    def _():
+        doc_copy.start()
+
+    with jax.named_scope("m_ldw"):
+        ld_sn.wait()
+        ld_wp.wait()
+    with jax.named_scope("m_rel"):
+        rel = dot(sn[...], wp[...]).astype(BF16)
+
+    def blocks_of(to):
+        for zz in range(4):
+            yield zz, pl.ds(pl.multiple_of((zz * 8 + to) * 128, 128), 128)
+
+    def share_weights():
+        for n, (xx, cc) in enumerate(((xr, c), (xl, c), (xr, 1 - c), (xl, 1 - c), (x, 1 - c))):
+            for zz, cols in blocks_of(xx * 2 + cc):
+                pltpu.make_async_remote_copy(
+                    src_ref=wout.at[:, cols],
+                    dst_ref=wo.at[xc, zz],
+                    send_sem=w_ss.at[n],
+                    recv_sem=w_rs.at[xc],
+                    device_id={"mp": mp_of(z, xx, cc)},
+                    device_id_type=MESH,
+                ).start()
+        for n, cc in enumerate((0, 1)):
+            for zz, cols in blocks_of(x_far * 2 + cc):
+                pltpu.make_async_remote_copy(
+                    src_ref=wout.at[:, cols],
+                    dst_ref=via.at[n, zz],
+                    send_sem=w_ss.at[5 + n],
+                    recv_sem=via_rs.at[n],
+                    device_id={"mp": mp_of(z, x_dn, c)},
+                    device_id_type=MESH,
+                ).start()
+        for zz, cols in blocks_of(xc):
+            pltpu.make_async_copy(wout.at[:, cols], wo.at[xc, zz], lsem.at[3]).start()
+
+    def via_copy(n):
+        slot = x_up * 2 + c
+        return pltpu.make_async_remote_copy(
+            src_ref=via.at[n],
+            dst_ref=wo.at[slot],
+            send_sem=via_ss.at[n],
+            recv_sem=w_rs.at[slot],
+            device_id={"mp": mp_of(z, x_dn, n)},
+            device_id_type=MESH,
+        )
+
+    def relay_weights():
+        for n in (0, 1):
+            pltpu.make_async_remote_copy(
+                src_ref=via.at[n],
+                dst_ref=via.at[n],
+                send_sem=via_ss.at[n],
+                recv_sem=via_rs.at[n],
+                device_id={"mp": me},
+                device_id_type=MESH,
+            ).wait_recv()
+            via_copy(n).start()
 
     def from_z(k):
         slot = mp_of(zo[k], x, c)
         landed(slot)
         push(toks.at[slot], slot, mp_of(z, xr, c))
         push(toks.at[slot], slot, mp_of(z, xl, c))
-        if k == 3:
+        if k >= 2:
             push(toks.at[slot], slot, mp_of(z, x_far, c))
         push(toks.at[slot], slot, mp_of(z, x, 1 - c))
 
     def from_x(k):
         slot = mp_of(zo[k], x_up, c)
         landed(slot)
-        if k < 3:
+        if k < 2:
             push(toks.at[slot], slot, mp_of(z, x_dn, c))
         push(toks.at[slot], slot, mp_of(z, x, 1 - c))
         slot = mp_of(zo[k], x_dn, c)
@@ -167,33 +228,32 @@
             acc[...] += term
 
     for k in (1, 2, 3):
-        from_z(k)
+        with jax.named_scope(f"m_z{k}"):
+            from_z(k)
     for k in (0, 1, 2, 3):
-        from_x(k)
-    for k in (0, 1, 2, 3):
-        from_far(k)
-
-    w_copies = []
-    for k in (1, 7, 2, 6, 3, 5, 4):
-        to = (xc + k) % 8
-        for zz in range(4):
-            cols = pl.ds(pl.multiple_of((zz * 8 + to) * 128, 128), 128)
-            pltpu.make_async_remote_copy(
-                src_ref=wout.at[:, cols],
-                dst_ref=wo.at[xc, zz],
-                send_sem=w_ss.at[k],
-                recv_sem=w_rs.at[xc],
-                device_id={"mp": z * 8 + to},
-                device_id_type=MESH,
-            ).start()
-    for zz in range(4):
-        cols = pl.ds(pl.multiple_of((zz * 8 + xc) * 128, 128), 128)
-        pltpu.make_async_copy(wout.at[:, cols], wo.at[xc, zz], lsem.at[3]).start()
+        with jax.named_scope(f"m_x{k}"):
+            from_x(k)
+
+    late = seq % 3 == 2
+
+    @pl.when(jnp.logical_not(late))
+    def _():
+        share_weights()
+
+    for k in (2, 3, 0, 1):
+        with jax.named_scope(f"m_far{k}"):
+            from_far(k)
+
+    @pl.when(late)
+    def _():
+        share_weights()
 
     ld_wv.wait()
     for k in (0, 1, 2, 3):
-        from_core(k)
-        project(k)
+        with jax.named_scope(f"m_core{k}"):
+            from_core(k)
+        with jax.named_scope(f"m_proj{k}"):
+            project(k)
 
     kvs[0] = acc[:, 128:256].astype(BF16)
     kvs[1] = acc[:, 256:384].astype(BF16)
@@ -207,8 +267,12 @@
             device_id={"seq": nxt},
             device_id_type=MESH,
         )
-        copy.start()
         kv_copies.append(copy)
+
+    @pl.when(has_next)
+    def _():
+        for copy in kv_copies:
+            copy.start()
 
     ld_cb.wait()
     ld_pb.wait()
@@ -226,9 +290,25 @@
     s_own = jnp.where(ok_own, s_own, F32(-1e30))
     top_own = jnp.max(s_own, axis=1, keepdims=True)
 
-    doc_copy.wait_recv()
+    @pl.when(has_prev)
+    def _():
+        doc_copy.wait_recv()
+
+    @pl.when(seq == 0)
+    def _():
+        docm[...] = jnp.zeros_like(docm)
+        kvm[...] = jnp.zeros_like(kvm)
+
     ok_mem = (row_doc == docm[...]) & (seq > 0)
-    kv_copies[0].wait_recv()
+    for copy in sends:
+        copy.wait_send()
+    with jax.named_scope("m_via"):
+        relay_weights()
+    with jax.named_scope("m_kv0"):
+
+        @pl.when(has_prev)
+        def _():
+            kv_copies[0].wait_recv()
     s_mem = (dot_t(qc, kvm[0]) + pos[:, 0:128]) * scale
     s_mem = jnp.where(ok_mem, s_mem, F32(-1e30))
     top = jnp.maximum(top_own, jnp.max(s_mem, axis=1, keepdims=True))
@@ -237,7 +317,11 @@
     total = jnp.sum(e_own, axis=1, keepdims=True) + jnp.sum(e_mem, axis=1, keepdims=True)
     w_own = (e_own / total).astype(BF16)
     w_mem = (e_mem / total).astype(BF16)
-    kv_copies[1].wait_recv()
+    with jax.named_scope("m_kv1"):
+
+        @pl.when(has_prev)
+        def _():
+            kv_copies[1].wait_recv()
     head = dot(w_own, kvs[1]) + dot(w_mem, kvm[1])
     ho[xc] = head.astype(BF16)
 
@@ -254,8 +338,7 @@
         copy.start()
         ho_copies.append(copy)
 
-    for k in range(1, 8):
-        slot = (xc + k) % 8
+    def weights_in(slot):
         pltpu.make_async_remote_copy(
             src_ref=wo.at[slot],
             dst_ref=wo.at[slot],
@@ -264,9 +347,8 @@
             device_id={"mp": me},
             device_id_type=MESH,
         ).wait_recv()
-    pltpu.make_async_copy(wo.at[xc], wo.at[xc], lsem.at[3]).wait()
-    for k in range(1, 8):
-        slot = (xc + k) % 8
+
+    def heads_in(slot):
         pltpu.make_async_remote_copy(
             src_ref=ho.at[slot],
             dst_ref=ho.at[slot],
@@ -276,12 +358,31 @@
             device_id_type=MESH,
         ).wait_recv()
 
-    heads = jnp.concatenate([ho[j] for j in range(8)], axis=1)
+    def pair_term(xs, zz):
+        slots = [xx * 2 + cc for xx in xs for cc in (0, 1)]
+        left = jnp.concatenate([ho[j] for j in slots], axis=1)
+        right = jnp.concatenate([wo[j, zz] for j in slots], axis=0)
+        return dot(left, right)
+
+    with jax.named_scope("m_wo"):
+        pltpu.make_async_copy(wo.at[xc], wo.at[xc], lsem.at[3]).wait()
+        for slot in (x * 2 + 1 - c, xr * 2, xr * 2 + 1, xl * 2, xl * 2 + 1):
+            weights_in(slot)
+    with jax.named_scope("m_ho"):
+        for slot in (x * 2 + 1 - c, xr * 2, xr * 2 + 1, xl * 2, xl * 2 + 1):
+            heads_in(slot)
+    for k in (3, 2, 1, 0):
+        part[zo[k]] = pair_term((x, xr, xl), zo[k])
+    with jax.named_scope("m_wof"):
+        for slot in (x_far * 2, x_far * 2 + 1):
+            weights_in(slot)
+    with jax.named_scope("m_hof"):
+        for slot in (x_far * 2, x_far * 2 + 1):
+            heads_in(slot)
     p_copies = []
     for k in (3, 2, 1, 0):
         zz = zo[k]
-        right = jnp.concatenate([wo[j, zz] for j in range(8)], axis=0)
-        part[zz] = dot(heads, right)
+        part[zz] += pair_term((x_far,), zz)
         if k > 0:
             copy = pltpu.make_async_remote_copy(
                 src_ref=part.at[zz],
@@ -293,33 +394,44 @@
             )
             copy.start()
             p_copies.append(copy)
+
+    for n in range(7):
+        pltpu.make_async_remote_copy(
+            src_ref=wo.at[xc],
+            dst_ref=wo.at[xc],
+            send_sem=w_ss.at[n],
+            recv_sem=w_rs.at[xc],
+            device_id={"mp": me},
+            device_id_type=MESH,
+        ).wait_send()
+    for n in (0, 1):
+        via_copy(n).wait_send()
+    for copy in ho_copies:
+        copy.wait_send()
+
+    @pl.when(has_next)
+    def _():
+        for copy in kv_copies + [doc_copy]:
+            copy.wait_send()
+
     result = part[z]
     for k in (1, 2, 3):
         zz = zo[k]
-        pltpu.make_async_remote_copy(
-            src_ref=rcv.at[zz],
-            dst_ref=rcv.at[zz],
-            send_sem=p_ss.at[0],
-            recv_sem=p_rs.at[zz],
-            device_id={"mp": me},
-            device_id_type=MESH,
-        ).wait_recv()
+        with jax.named_scope(f"m_part{k}"):
+            pltpu.make_async_remote_copy(
+                src_ref=rcv.at[zz],
+                dst_ref=rcv.at[zz],
+                send_sem=p_ss.at[0],
+                recv_sem=p_rs.at[zz],
+                device_id={"mp": me},
+                device_id_type=MESH,
+            ).wait_recv()
         result = result + rcv[zz]
     out[...] = result.astype(BF16)
 
-    for copy in sends:
-        copy.wait_send()
-    for k in range(1, 8):
-        pltpu.make_async_remote_copy(
-            src_ref=wo.at[xc],
-            dst_ref=wo.at[xc],
-            send_sem=w_ss.at[k],
-            recv_sem=w_rs.at[xc],
-            device_id={"mp": me},
-            device_id_type=MESH,
-        ).wait_send()
-    for copy in kv_copies + [doc_copy] + ho_copies + p_copies:
-        copy.wait_send()
+    with jax.named_scope("m_send"):
+        for copy in p_copies:
+            copy.wait_send()
 
 
 def shards(tokens, w_qkv, w_pos, w_out, content_bias, position_bias, doc_ids):
@@ -351,6 +463,9 @@
             pltpu.VMEM((8, 128, 128), BF16),
             pltpu.VMEM((4, 128, 128), F32),
             pltpu.VMEM((4, 128, 128), F32),
+            pltpu.VMEM((2, 4, 128, 128), BF16),
+            pltpu.SemaphoreType.DMA((2,)),
+            pltpu.SemaphoreType.DMA((2,)),
             pltpu.SemaphoreType.DMA((8,)),
             pltpu.SemaphoreType.DMA((31,)),
             pltpu.SemaphoreType.DMA((32,)),

time: 51.1 us -> 49.2 us (0.963)
  the two profiles are of different devices: /device:TPU:6 before, /device:TPU:56 now
where the time goes in v1:
time: 49.2 us; the launch traced here: 49.1 us
  Pallas kernels  48.4 us (98%)
  local copies, waits for them, and re-layouts  0.62 us (1%)
    pallas_call x1, Pallas kernels, shards(): pl.pallas_call(kernel, out_shape=pltpu.VMEM((128, 128), BF16), in_specs=[...  48.4 us

profile of v1, /device:TPU:56, one launch (start us, length us, event | category | flops | bytes accessed | tf_op | source)
XLA Modules:
  0.0 49.1 jit_solution(1834017664530984463)
XLA Ops:
  0.0 48.4 %layer.1 = bf16[128,128]{1,0:T(8,128)(2,1)S(1)} custom-call(bf16[128,128]{1,0:T(8,128)(2,1)} %tok_in.1, bf16[3,4096,128]{2,1,0:T(8,128)(2,1)} %wqkv.1, bf16[4096,128]{1,0:T(8,128)(2,1)} %wpos.1, bf16[128,4096]{1,0:T(8,128)(2,1)} %wout.1, f32[1,128]{1,0:T(1,128)} %cbias_in.1, f32[1,128]{1,0:T(1,128)} %pbias_in.1, s32[1,128]{1,0:T(1,128)} %bitcast.1, ...), custom_call_target="tpu_custom_call" | custom-call | tf_op jit(solution)/shard_map/layer/pallas_call | solution.py:445
  48.4 0.6 %copy.10 = bf16[128,128]{1,0:T(8,128)(2,1)} copy(bf16[128,128]{1,0:T(8,128)(2,1)S(1)} %layer.1) | data formatting | bytes 65536

commit v2 on v1

--- a/solution.py
+++ b/solution.py
@@ -9,6 +9,7 @@
 MESH = pl.DeviceIdType.MESH
 F32 = jnp.float32
 BF16 = jnp.bfloat16
+BANDS = 2
 
 
 def sinus_reversed(count, width):
@@ -32,7 +33,7 @@
 def kernel(
     tok_in, wqkv, wpos, wout, cbias_in, pbias_in, doc_in, sinus, out,
     cbias, pbias, doc, toks, wv, wp, sn, wo, acc, kvs, kvm, docm, ho, part, rcv,
-    via, via_ss, via_rs, lsem, tok_ss, tok_rs, w_ss, w_rs, kv_ss, kv_rs, ho_ss, ho_rs, p_ss, p_rs,
+    wst, via, ready, via_ss, via_rs, lsem, tok_ss, tok_rs, w_ss, w_rs, kv_ss, kv_rs, ho_ss, ho_rs, p_ss, p_rs,
 ):
     seq = lax.axis_index("seq")
     me = lax.axis_index("mp")
@@ -40,6 +41,7 @@
     z, x, c = me // 8, (me // 2) % 4, me % 2
     xc = me % 8
     nxt, prv = (seq + 1) % n_seq, (seq + n_seq - 1) % n_seq
+    turn = seq % 3
     has_next, has_prev = seq < n_seq - 1, seq > 0
     xr, xl = (x + 1) % 4, (x + 3) % 4
     dirn = 1 - 2 * c
@@ -48,6 +50,8 @@
     inner = (z // 2 + z % 2) % 2
     za, zb, zc = z + 1 - 2 * (z % 2), 3 - z, (z + 2) % 4
     zo = [z, za, inner * zb + (1 - inner) * zc, inner * zc + (1 - inner) * zb]
+
+    peers = [(xr, c), (xl, c), (xr, 1 - c), (xl, 1 - c), (x, 1 - c), (x_far, c), (x_far, 1 - c)]
 
     def mp_of(zz, xx, cc):
         return (zz * 4 + xx) * 2 + cc
@@ -61,9 +65,13 @@
         pl.semaphore_signal(
             barrier, inc=1, device_id={"mp": mp_of(zo[k], x, c)}, device_id_type=MESH
         )
-    @pl.when(has_prev)
+    @pl.when(has_prev & (turn == 0))
     def _():
         pl.semaphore_signal(barrier, inc=1, device_id={"seq": prv}, device_id_type=MESH)
+
+    @pl.when(turn != 2)
+    def _():
+        pl.semaphore_signal(barrier, inc=1, device_id={"seq": nxt}, device_id_type=MESH)
 
     ld_tok = pltpu.make_async_copy(tok_in, toks.at[me], lsem.at[4])
     ld_tok.start()
@@ -79,13 +87,23 @@
     ld_sn.start()
     ld_wp.start()
     ld_wv.start()
+    for to in range(8):
+        for zz in range(4):
+            cols = pl.ds((zz * 8 + to) * 128, 128)
+            pltpu.make_async_copy(wout.at[:, cols], wst.at[to, zz], lsem.at[8]).start()
     tok = toks.at[me]
     with jax.named_scope("m_tok"):
         ld_tok.wait()
         ld_doc.wait()
 
     with jax.named_scope("m_bar"):
-        pl.semaphore_wait(barrier, 10 + has_next.astype(jnp.int32))
+        heard = (turn != 0).astype(jnp.int32) + (has_next & (turn == 2)).astype(jnp.int32)
+        pl.semaphore_wait(barrier, 10 + heard)
+
+    @pl.when(turn != 0)
+    def _():
+        pl.semaphore_signal(ready, inc=1, device_id={"seq": prv}, device_id_type=MESH)
+
 
     sends = []
 
@@ -115,6 +133,7 @@
     push(tok, me, mp_of(zo[1], x, c))
     push(tok, me, mp_of(z, xr, c))
     push(tok, me, mp_of(z, xl, c))
+    push(tok, me, mp_of(z, x_far, c))
     push(tok, me, mp_of(zo[2], x, c))
     push(tok, me, mp_of(zo[3], x, c))
     push(tok, me, mp_of(z, x, 1 - c))
@@ -127,7 +146,7 @@
         device_id_type=MESH,
     )
 
-    @pl.when(has_next)
+    @pl.when(has_next & (turn == 2))
     def _():
         doc_copy.start()
 
@@ -137,33 +156,27 @@
     with jax.named_scope("m_rel"):
         rel = dot(sn[...], wp[...]).astype(BF16)
 
-    def blocks_of(to):
-        for zz in range(4):
-            yield zz, pl.ds(pl.multiple_of((zz * 8 + to) * 128, 128), 128)
-
     def share_weights():
-        for n, (xx, cc) in enumerate(((xr, c), (xl, c), (xr, 1 - c), (xl, 1 - c), (x, 1 - c))):
-            for zz, cols in blocks_of(xx * 2 + cc):
-                pltpu.make_async_remote_copy(
-                    src_ref=wout.at[:, cols],
-                    dst_ref=wo.at[xc, zz],
-                    send_sem=w_ss.at[n],
-                    recv_sem=w_rs.at[xc],
-                    device_id={"mp": mp_of(z, xx, cc)},
-                    device_id_type=MESH,
-                ).start()
+        pltpu.make_async_copy(wst, wst, lsem.at[8]).wait()
         for n, cc in enumerate((0, 1)):
-            for zz, cols in blocks_of(x_far * 2 + cc):
-                pltpu.make_async_remote_copy(
-                    src_ref=wout.at[:, cols],
-                    dst_ref=via.at[n, zz],
-                    send_sem=w_ss.at[5 + n],
-                    recv_sem=via_rs.at[n],
-                    device_id={"mp": mp_of(z, x_dn, c)},
-                    device_id_type=MESH,
-                ).start()
-        for zz, cols in blocks_of(xc):
-            pltpu.make_async_copy(wout.at[:, cols], wo.at[xc, zz], lsem.at[3]).start()
+            pltpu.make_async_remote_copy(
+                src_ref=wst.at[x_far * 2 + cc],
+                dst_ref=via.at[n],
+                send_sem=w_ss.at[5 + n],
+                recv_sem=via_rs.at[n],
+                device_id={"mp": mp_of(z, x_dn, c)},
+                device_id_type=MESH,
+            ).start()
+        for n, (xx, cc) in enumerate(peers[:5]):
+            pltpu.make_async_remote_copy(
+                src_ref=wst.at[xx * 2 + cc],
+                dst_ref=wo.at[xc],
+                send_sem=w_ss.at[n],
+                recv_sem=w_rs.at[xc],
+                device_id={"mp": mp_of(z, xx, cc)},
+                device_id_type=MESH,
+            ).start()
+        pltpu.make_async_copy(wst.at[xc], wo.at[xc], lsem.at[3]).start()
 
     def via_copy(n):
         slot = x_up * 2 + c
@@ -193,15 +206,11 @@
         landed(slot)
         push(toks.at[slot], slot, mp_of(z, xr, c))
         push(toks.at[slot], slot, mp_of(z, xl, c))
-        if k >= 2:
-            push(toks.at[slot], slot, mp_of(z, x_far, c))
         push(toks.at[slot], slot, mp_of(z, x, 1 - c))
 
     def from_x(k):
         slot = mp_of(zo[k], x_up, c)
         landed(slot)
-        if k < 2:
-            push(toks.at[slot], slot, mp_of(z, x_dn, c))
         push(toks.at[slot], slot, mp_of(z, x, 1 - c))
         slot = mp_of(zo[k], x_dn, c)
         landed(slot)
@@ -210,50 +219,54 @@
     def from_far(k):
         slot = mp_of(zo[k], x_far, c)
         landed(slot)
+        if k == 0:
+            for j in (1, 2, 3):
+                push(toks.at[slot], slot, mp_of(zo[j], x, c))
         push(toks.at[slot], slot, mp_of(z, x, 1 - c))
 
     def from_core(k):
         for xx in (x, x_up, x_dn, x_far):
             landed(mp_of(zo[k], xx, 1 - c))
 
-    def project(k):
-        zz = zo[k]
-        left = jnp.concatenate([toks[zz * 8 + j] for j in range(8)], axis=1)
-        rows = pl.ds(pl.multiple_of(zz * 1024, 1024), 1024)
-        right = jnp.concatenate([wv[0, rows, :], wv[1, rows, :], wv[2, rows, :]], axis=1)
-        term = dot(left, right)
-        if k == 0:
-            acc[...] = term
-        else:
-            acc[...] += term
-
+    def project(k, cc):
+        slots = [mp_of(zo[k], xx, cc) for xx in range(4)]
+        left = jnp.concatenate([toks[j] for j in slots], axis=1)
+        bands = [pl.ds(pl.multiple_of(j * 128, 128), 128) for j in slots]
+        right = jnp.concatenate(
+            [jnp.concatenate([wv[i, band, :] for band in bands], axis=0) for i in range(3)], axis=1
+        )
+        return dot(left, right)
+
+    def at(name, step, k):
+        with jax.named_scope(f"m_{name}{k}"):
+            step(k)
+
+    at("z", from_z, 1)
+    at("z", from_z, 2)
+    at("far", from_far, 0)
+    at("z", from_z, 3)
+
+    @pl.when(turn != 2)
+    def _():
+        share_weights()
+
+    at("x", from_x, 0)
     for k in (1, 2, 3):
-        with jax.named_scope(f"m_z{k}"):
-            from_z(k)
+        at("x", from_x, k)
+        at("far", from_far, k)
+
+    @pl.when(turn == 2)
+    def _():
+        share_weights()
+
+    ld_wv.wait()
+    with jax.named_scope("m_same"):
+        acc[...] = project(0, c)
+        for k in (1, 2, 3):
+            acc[...] += project(k, c)
     for k in (0, 1, 2, 3):
-        with jax.named_scope(f"m_x{k}"):
-            from_x(k)
-
-    late = seq % 3 == 2
-
-    @pl.when(jnp.logical_not(late))
-    def _():
-        share_weights()
-
-    for k in (2, 3, 0, 1):
-        with jax.named_scope(f"m_far{k}"):
-            from_far(k)
-
-    @pl.when(late)
-    def _():
-        share_weights()
-
-    ld_wv.wait()
-    for k in (0, 1, 2, 3):
-        with jax.named_scope(f"m_core{k}"):
-            from_core(k)
-        with jax.named_scope(f"m_proj{k}"):
-            project(k)
+        at("core", from_core, k)
+        acc[...] += project(k, 1 - c)
 
     kvs[0] = acc[:, 128:256].astype(BF16)
     kvs[1] = acc[:, 256:384].astype(BF16)
@@ -269,7 +282,15 @@
         )
         kv_copies.append(copy)
 
-    @pl.when(has_next)
+    @pl.when(turn != 2)
+    def _():
+        pl.semaphore_wait(ready, 1)
+
+    @pl.when(turn != 2)
+    def _():
+        doc_copy.start()
+
+    @pl.when(has_next & (turn != 1))
     def _():
         for copy in kv_copies:
             copy.start()
@@ -290,20 +311,22 @@
     s_own = jnp.where(ok_own, s_own, F32(-1e30))
     top_own = jnp.max(s_own, axis=1, keepdims=True)
 
-    @pl.when(has_prev)
-    def _():
-        doc_copy.wait_recv()
-
-    @pl.when(seq == 0)
-    def _():
-        docm[...] = jnp.zeros_like(docm)
-        kvm[...] = jnp.zeros_like(kvm)
-
-    ok_mem = (row_doc == docm[...]) & (seq > 0)
     for copy in sends:
         copy.wait_send()
     with jax.named_scope("m_via"):
         relay_weights()
+
+    @pl.when(has_prev)
+    def _():
+        doc_copy.wait_recv()
+
+    @pl.when(seq == 0)
+    def _():
+        docm[...] = jnp.zeros_like(docm)
+        kvm[...] = jnp.zeros_like(kvm)
+
+    ok_mem = (row_doc == docm[...]) & (seq > 0)
+
     with jax.named_scope("m_kv0"):
 
         @pl.when(has_prev)
@@ -322,21 +345,26 @@
         @pl.when(has_prev)
         def _():
             kv_copies[1].wait_recv()
-    head = dot(w_own, kvs[1]) + dot(w_mem, kvm[1])
-    ho[xc] = head.astype(BF16)
-
+
+    rows_in = 128 // BANDS
     ho_copies = []
-    for k in (1, 7, 2, 6, 3, 5, 4):
-        copy = pltpu.make_async_remote_copy(
-            src_ref=ho.at[xc],
-            dst_ref=ho.at[xc],
-            send_sem=ho_ss.at[k],
-            recv_sem=ho_rs.at[xc],
-            device_id={"mp": z * 8 + (xc + k) % 8},
-            device_id_type=MESH,
-        )
-        copy.start()
-        ho_copies.append(copy)
+    for half in range(BANDS):
+        band = slice(half * rows_in, half * rows_in + rows_in)
+        head = dot(w_own[band], kvs[1]) + dot(w_mem[band], kvm[1])
+        ho[half, xc] = head.astype(BF16)
+        for copy in ho_copies[-7:]:
+            copy.wait_send()
+        for n, (xx, cc) in enumerate(peers):
+            copy = pltpu.make_async_remote_copy(
+                src_ref=ho.at[half, xc],
+                dst_ref=ho.at[half, xc],
+                send_sem=ho_ss.at[half, n],
+                recv_sem=ho_rs.at[half, xc],
+                device_id={"mp": mp_of(z, xx, cc)},
+                device_id_type=MESH,
+            )
+            copy.start()
+            ho_copies.append(copy)
 
     def weights_in(slot):
         pltpu.make_async_remote_copy(
@@ -348,52 +376,58 @@
             device_id_type=MESH,
         ).wait_recv()
 
-    def heads_in(slot):
+    def heads_in(half, slot):
         pltpu.make_async_remote_copy(
-            src_ref=ho.at[slot],
-            dst_ref=ho.at[slot],
-            send_sem=ho_ss.at[0],
-            recv_sem=ho_rs.at[slot],
+            src_ref=ho.at[half, slot],
+            dst_ref=ho.at[half, slot],
+            send_sem=ho_ss.at[half, 0],
+            recv_sem=ho_rs.at[half, slot],
             device_id={"mp": me},
             device_id_type=MESH,
         ).wait_recv()
 
-    def pair_term(xs, zz):
+    def term(half, xs, zz):
         slots = [xx * 2 + cc for xx in xs for cc in (0, 1)]
-        left = jnp.concatenate([ho[j] for j in slots], axis=1)
+        left = jnp.concatenate([ho[half, j] for j in slots], axis=1)
         right = jnp.concatenate([wo[j, zz] for j in slots], axis=0)
         return dot(left, right)
 
+    near = (x * 2 + 1 - c, xr * 2, xr * 2 + 1, xl * 2, xl * 2 + 1)
+    far = (x_far * 2, x_far * 2 + 1)
     with jax.named_scope("m_wo"):
         pltpu.make_async_copy(wo.at[xc], wo.at[xc], lsem.at[3]).wait()
-        for slot in (x * 2 + 1 - c, xr * 2, xr * 2 + 1, xl * 2, xl * 2 + 1):
+        for slot in near + far:
             weights_in(slot)
-    with jax.named_scope("m_ho"):
-        for slot in (x * 2 + 1 - c, xr * 2, xr * 2 + 1, xl * 2, xl * 2 + 1):
-            heads_in(slot)
-    for k in (3, 2, 1, 0):
-        part[zo[k]] = pair_term((x, xr, xl), zo[k])
-    with jax.named_scope("m_wof"):
-        for slot in (x_far * 2, x_far * 2 + 1):
-            weights_in(slot)
-    with jax.named_scope("m_hof"):
-        for slot in (x_far * 2, x_far * 2 + 1):
-            heads_in(slot)
+
+    @pl.when(turn == 1)
+    def _():
+        for copy in kv_copies:
+            copy.start()
+
     p_copies = []
-    for k in (3, 2, 1, 0):
-        zz = zo[k]
-        part[zz] += pair_term((x_far,), zz)
-        if k > 0:
-            copy = pltpu.make_async_remote_copy(
-                src_ref=part.at[zz],
-                dst_ref=rcv.at[z],
-                send_sem=p_ss.at[k],
-                recv_sem=p_rs.at[z],
-                device_id={"mp": mp_of(zz, x, c)},
-                device_id_type=MESH,
-            )
-            copy.start()
-            p_copies.append(copy)
+    for half in range(BANDS):
+        with jax.named_scope(f"m_ho{half}"):
+            for slot in near:
+                heads_in(half, slot)
+        for k in (3, 2, 1, 0):
+            part[half, zo[k]] = term(half, (x, xr, xl), zo[k])
+        with jax.named_scope(f"m_hof{half}"):
+            for slot in far:
+                heads_in(half, slot)
+        for k in (3, 2, 1, 0):
+            zz = zo[k]
+            part[half, zz] += term(half, (x_far,), zz)
+            if k > 0:
+                copy = pltpu.make_async_remote_copy(
+                    src_ref=part.at[half, zz],
+                    dst_ref=rcv.at[half, z],
+                    send_sem=p_ss.at[half, k],
+                    recv_sem=p_rs.at[half, z],
+                    device_id={"mp": mp_of(zz, x, c)},
+                    device_id_type=MESH,
+                )
+                copy.start()
+                p_copies.append(copy)
 
     for n in range(7):
         pltpu.make_async_remote_copy(
@@ -406,7 +440,7 @@
         ).wait_send()
     for n in (0, 1):
         via_copy(n).wait_send()
-    for copy in ho_copies:
+    for copy in ho_copies[-7:]:
         copy.wait_send()
 
     @pl.when(has_next)
@@ -414,20 +448,21 @@
         for copy in kv_copies + [doc_copy]:
             copy.wait_send()
 
-    result = part[z]
-    for k in (1, 2, 3):
-        zz = zo[k]
-        with jax.named_scope(f"m_part{k}"):
-            pltpu.make_async_remote_copy(
-                src_ref=rcv.at[zz],
-                dst_ref=rcv.at[zz],
-                send_sem=p_ss.at[0],
-                recv_sem=p_rs.at[zz],
-                device_id={"mp": me},
-                device_id_type=MESH,
-            ).wait_recv()
-        result = result + rcv[zz]
-    out[...] = result.astype(BF16)
+    for half in range(BANDS):
+        result = part[half, z]
+        for k in (1, 2, 3):
+            zz = zo[k]
+            with jax.named_scope(f"m_part{half}{k}"):
+                pltpu.make_async_remote_copy(
+                    src_ref=rcv.at[half, zz],
+                    dst_ref=rcv.at[half, zz],
+                    send_sem=p_ss.at[half, 0],
+                    recv_sem=p_rs.at[half, zz],
+                    device_id={"mp": me},
+                    device_id_type=MESH,
+                ).wait_recv()
+            result = result + rcv[half, zz]
+        out[half * rows_in : half * rows_in + rows_in, :] = result.astype(BF16)
 
     with jax.named_scope("m_send"):
         for copy in p_copies:
@@ -460,23 +495,25 @@
             pltpu.VMEM((2, 128, 128), BF16),
             pltpu.VMEM((2, 128, 128), BF16),
             pltpu.VMEM((1, 128), jnp.int32),
-            pltpu.VMEM((8, 128, 128), BF16),
-            pltpu.VMEM((4, 128, 128), F32),
-            pltpu.VMEM((4, 128, 128), F32),
+            pltpu.VMEM((BANDS, 8, 128 // BANDS, 128), BF16),
+            pltpu.VMEM((BANDS, 4, 128 // BANDS, 128), F32),
+            pltpu.VMEM((BANDS, 4, 128 // BANDS, 128), F32),
+            pltpu.VMEM((8, 4, 128, 128), BF16),
             pltpu.VMEM((2, 4, 128, 128), BF16),
+            pltpu.SemaphoreType.REGULAR,
             pltpu.SemaphoreType.DMA((2,)),
             pltpu.SemaphoreType.DMA((2,)),
-            pltpu.SemaphoreType.DMA((8,)),
+            pltpu.SemaphoreType.DMA((9,)),
             pltpu.SemaphoreType.DMA((31,)),
             pltpu.SemaphoreType.DMA((32,)),
             pltpu.SemaphoreType.DMA((8,)),
             pltpu.SemaphoreType.DMA((8,)),
             pltpu.SemaphoreType.DMA((3,)),
             pltpu.SemaphoreType.DMA((3,)),
-            pltpu.SemaphoreType.DMA((8,)),
-            pltpu.SemaphoreType.DMA((8,)),
-            pltpu.SemaphoreType.DMA((4,)),
-            pltpu.SemaphoreType.DMA((4,)),
+            pltpu.SemaphoreType.DMA((BANDS, 7)),
+            pltpu.SemaphoreType.DMA((BANDS, 8)),
+            pltpu.SemaphoreType.DMA((BANDS, 4)),
+            pltpu.SemaphoreType.DMA((BANDS, 4)),
         ],
         compiler_params=pltpu.CompilerParams(
             collective_id=0, has_side_effects=True, vmem_limit_bytes=20 * 1024 * 1024

time: 49.2 us -> 47.9 us (0.974)
  Pallas kernels: 48.4 us -> 47.2 us
    pallas_call x1, Pallas kernels: 48.4 us -> 47.2 us  [shards(): pl.pallas_call(kernel, out_shape=pltpu.VMEM((128, 128), BF16), in_specs=[...]
where the time goes in v2:
time: 47.9 us; the launch traced here: 47.8 us
  Pallas kernels  47.2 us (99%)
  local copies, waits for them, and re-layouts  0.62 us (1%)
    pallas_call x1, Pallas kernels, shards(): pl.pallas_call(kernel, out_shape=pltpu.VMEM((128, 128), BF16), in_specs=[...  47.2 us

profile of v2, /device:TPU:56, one launch (start us, length us, event | category | flops | bytes accessed | tf_op | source)
XLA Modules:
  0.0 47.8 jit_solution(10850837595709287438)
XLA Ops:
  0.0 47.2 %layer.1 = bf16[128,128]{1,0:T(8,128)(2,1)S(1)} custom-call(bf16[128,128]{1,0:T(8,128)(2,1)} %tok_in.1, bf16[3,4096,128]{2,1,0:T(8,128)(2,1)} %wqkv.1, bf16[4096,128]{1,0:T(8,128)(2,1)} %wpos.1, bf16[128,4096]{1,0:T(8,128)(2,1)} %wout.1, f32[1,128]{1,0:T(1,128)} %cbias_in.1, f32[1,128]{1,0:T(1,128)} %pbias_in.1, s32[1,128]{1,0:T(1,128)} %bitcast.1, ...), custom_call_target="tpu_custom_call" | custom-call | tf_op jit(solution)/shard_map/layer/pallas_call | solution.py:480
  47.2 0.6 %copy.10 = bf16[128,128]{1,0:T(8,128)(2,1)} copy(bf16[128,128]{1,0:T(8,128)(2,1)S(1)} %layer.1) | data formatting | bytes 65536

commit v3 on v2

v3 whole, which is shorter than its diff:
```python
import jax
import jax.numpy as jnp
import numpy as np
from jax import lax
from jax.experimental import pallas as pl
from jax.experimental.pallas import tpu as pltpu
from jax.sharding import PartitionSpec as P

MESH = pl.DeviceIdType.MESH
F32 = jnp.float32
BF16 = jnp.bfloat16
BANDS = 2


def sinus_reversed(count, width):
    place = np.arange(count, dtype=np.float32)[::-1, None]
    freqs = np.float32(1.0) / np.power(
        np.float32(10000.0), np.arange(0, width, 2, dtype=np.float32) / np.float32(width)
    )
    angle = place * freqs[None, :].astype(np.float32)
    table = np.concatenate([np.sin(angle), np.cos(angle)], axis=1)
    return table.astype(jnp.bfloat16)


def dot(a, b):
    return jnp.dot(a, b, preferred_element_type=F32)


def dot_t(a, b):
    return lax.dot_general(a, b, (((1,), (1,)), ((), ())), preferred_element_type=F32)


def kernel(
    tok_in, wqkv, wpos, wout, cbias_in, pbias_in, doc_in, sinus, out,
    cbias, pbias, doc, toks, wv, wp, sn, wo, acc, kvs, kvm, docm, ho, part, rcv,
    wst, via, ready, via_ss, via_rs, lsem, tok_ss, tok_rs, core_rs, w_ss, w_rs, kv_ss, kv_rs, ho_ss, ho_rs, p_ss, p_rs,
):
    seq = lax.axis_index("seq")
    me = lax.axis_index("mp")
    n_seq = lax.axis_size("seq")
    z, x, c = me // 8, (me // 2) % 4, me % 2
    xc = me % 8
    nxt, prv = (seq + 1) % n_seq, (seq + n_seq - 1) % n_seq
    turn = seq % 3
    has_next, has_prev = seq < n_seq - 1, seq > 0
    xr, xl = (x + 1) % 4, (x + 3) % 4
    dirn = 1 - 2 * c
    x_up, x_dn = (x - dirn + 4) % 4, (x + dirn + 4) % 4
    x_far = (x + 2) % 4
    inner = (z // 2 + z % 2) % 2
    za, zb, zc = z + 1 - 2 * (z % 2), 3 - z, (z + 2) % 4
    zo = [z, za, inner * zb + (1 - inner) * zc, inner * zc + (1 - inner) * zb]

    peers = [(xr, c), (xl, c), (xr, 1 - c), (xl, 1 - c), (x, 1 - c), (x_far, c), (x_far, 1 - c)]

    def mp_of(zz, xx, cc):
        return (zz * 4 + xx) * 2 + cc

    barrier = pltpu.get_barrier_semaphore()
    for k in range(1, 8):
        pl.semaphore_signal(
            barrier, inc=1, device_id={"mp": z * 8 + (xc + k) % 8}, device_id_type=MESH
        )
    for k in range(1, 4):
        pl.semaphore_signal(
            barrier, inc=1, device_id={"mp": mp_of(zo[k], x, c)}, device_id_type=MESH
        )
    @pl.when(has_prev & (turn == 0))
    def _():
        pl.semaphore_signal(barrier, inc=1, device_id={"seq": prv}, device_id_type=MESH)

    @pl.when(turn != 2)
    def _():
        pl.semaphore_signal(barrier, inc=1, device_id={"seq": nxt}, device_id_type=MESH)

    ld_tok = [
        pltpu.make_async_copy(tok_in.at[pl.ds(h * 64, 64)], toks.at[h, me], lsem.at[9 + h])
        for h in (0, 1)
    ]
    for copy in ld_tok:
        copy.start()
    ld_doc = pltpu.make_async_copy(doc_in, doc, lsem.at[5])
    ld_doc.start()
    ld_cb = pltpu.make_async_copy(cbias_in, cbias, lsem.at[6])
    ld_cb.start()
    ld_pb = pltpu.make_async_copy(pbias_in, pbias, lsem.at[7])
    ld_pb.start()
    ld_sn = pltpu.make_async_copy(sinus, sn, lsem.at[0])
    ld_wp = pltpu.make_async_copy(wpos, wp, lsem.at[1])
    ld_wv = pltpu.make_async_copy(wqkv, wv, lsem.at[2])
    ld_sn.start()
    ld_wp.start()
    ld_wv.start()
    with jax.named_scope("m_tok"):
        for copy in ld_tok:
            copy.wait()
        ld_doc.wait()

    with jax.named_scope("m_bar"):
        heard = (turn != 0).astype(jnp.int32) + (has_next & (turn == 2)).astype(jnp.int32)
        pl.semaphore_wait(barrier, 10 + heard)

    @pl.when(turn != 0)
    def _():
        pl.semaphore_signal(ready, inc=1, device_id={"seq": prv}, device_id_type=MESH)


    sends = [0, 0]

    def sent(all_of, sem):
        pltpu.make_async_remote_copy(
            src_ref=all_of,
            dst_ref=all_of,
            send_sem=sem,
            recv_sem=via_rs.at[0],
            device_id={"mp": me},
            device_id_type=MESH,
        ).wait_send()

    def arrived(all_of, sem):
        pltpu.make_async_remote_copy(
            src_ref=all_of,
            dst_ref=all_of,
            send_sem=via_ss,
            recv_sem=sem,
            device_id={"mp": me},
            device_id_type=MESH,
        ).wait_recv()

    def push(h, slot, target, partner=False):
        copy = pltpu.make_async_remote_copy(
            src_ref=toks.at[h, slot],
            dst_ref=toks.at[h, slot],
            send_sem=tok_ss.at[h],
            recv_sem=core_rs.at[h, slot // 8] if partner else tok_rs.at[h, slot // 2],
            device_id={"mp": target},
            device_id_type=MESH,
        )
        copy.start()
        sends[h] += 1

    def landed(h, slot):
        pltpu.make_async_remote_copy(
            src_ref=toks.at[h, slot],
            dst_ref=toks.at[h, slot],
            send_sem=tok_ss.at[h],
            recv_sem=tok_rs.at[h, slot // 2],
            device_id={"mp": me},
            device_id_type=MESH,
        ).wait_recv()

    def own(h):
        push(h, me, mp_of(zo[1], x, c))
        push(h, me, mp_of(z, xr, c))
        push(h, me, mp_of(z, xl, c))
        push(h, me, mp_of(z, x_far, c))
        push(h, me, mp_of(zo[2], x, c))
        push(h, me, mp_of(zo[3], x, c))
        push(h, me, mp_of(z, x, 1 - c), True)

    own(0)
    for to in range(8):
        for zz in range(4):
            cols = pl.ds((zz * 8 + to) * 128, 128)
            pltpu.make_async_copy(wout.at[:, cols], wst.at[to, zz], lsem.at[8]).start()
    doc_copy = pltpu.make_async_remote_copy(
        src_ref=doc,
        dst_ref=docm,
        send_sem=kv_ss.at[4],
        recv_sem=kv_rs.at[4],
        device_id={"seq": nxt},
        device_id_type=MESH,
    )

    @pl.when(has_next & (turn == 2))
    def _():
        doc_copy.start()

    with jax.named_scope("m_ldw"):
        ld_sn.wait()
        ld_wp.wait()
    with jax.named_scope("m_rel"):
        rel = dot(sn[...], wp[...]).astype(BF16)
    own(1)

    def share_weights():
        pltpu.make_async_copy(wst, wst, lsem.at[8]).wait()
        for n, cc in enumerate((0, 1)):
            pltpu.make_async_remote_copy(
                src_ref=wst.at[x_far * 2 + cc],
                dst_ref=via.at[n],
                send_sem=w_ss,
                recv_sem=via_rs.at[n],
                device_id={"mp": mp_of(z, x_dn, c)},
                device_id_type=MESH,
            ).start()
        for n, (xx, cc) in enumerate(peers[:5]):
            pltpu.make_async_remote_copy(
                src_ref=wst.at[xx * 2 + cc],
                dst_ref=wo.at[xc],
                send_sem=w_ss,
                recv_sem=w_rs,
                device_id={"mp": mp_of(z, xx, cc)},
                device_id_type=MESH,
            ).start()
        pltpu.make_async_copy(wst.at[xc], wo.at[xc], lsem.at[3]).start()

    def via_copy(n):
        slot = x_up * 2 + c
        return pltpu.make_async_remote_copy(
            src_ref=via.at[n],
            dst_ref=wo.at[slot],
            send_sem=via_ss,
            recv_sem=w_rs,
            device_id={"mp": mp_of(z, x_dn, n)},
            device_id_type=MESH,
        )

    def relay_weights():
        for n in (0, 1):
            arrived(via.at[n], via_rs.at[n])
            via_copy(n).start()

    def from_z(h, k):
        slot = mp_of(zo[k], x, c)
        landed(h, slot)
        push(h, slot, mp_of(z, xr, c))
        push(h, slot, mp_of(z, xl, c))
        push(h, slot, mp_of(z, x, 1 - c), True)

    def from_x(h, k):
        for xx in (x_up, x_dn):
            slot = mp_of(zo[k], xx, c)
            landed(h, slot)
            push(h, slot, mp_of(z, x, 1 - c), True)

    def from_far(h, k):
        slot = mp_of(zo[k], x_far, c)
        landed(h, slot)
        if k == 0:
            for j in (1, 2, 3):
                push(h, slot, mp_of(zo[j], x, c))
        push(h, slot, mp_of(z, x, 1 - c), True)

    def from_core(h, k):
        four = toks.at[h, pl.ds(0, 4)]
        pltpu.make_async_remote_copy(
            src_ref=four,
            dst_ref=four,
            send_sem=tok_ss.at[h],
            recv_sem=core_rs.at[h, zo[k]],
            device_id={"mp": me},
            device_id_type=MESH,
        ).wait_recv()

    def project(h, k, cc):
        slots = [mp_of(zo[k], xx, cc) for xx in range(4)]
        left = jnp.concatenate([toks[h, j] for j in slots], axis=1)
        bands = [pl.ds(pl.multiple_of(j * 128, 128), 128) for j in slots]
        right = jnp.concatenate(
            [jnp.concatenate([wv[i, band, :] for band in bands], axis=0) for i in range(3)], axis=1
        )
        return dot(left, right)

    def at(name, step, h, k):
        with jax.named_scope(f"m_{name}{h}{k}"):
            step(h, k)

    def across(h):
        at("z", from_z, h, 1)
        at("z", from_z, h, 2)
        at("far", from_far, h, 0)
        at("z", from_z, h, 3)

    def along(h, ks):
        for k in ks:
            at("x", from_x, h, k)
            if k > 0:
                at("far", from_far, h, k)

    def same(h):
        half = slice(h * 64, h * 64 + 64)
        with jax.named_scope(f"m_same{h}"):
            acc[half] = project(h, 0, c)
            for k in (1, 2, 3):
                acc[half] += project(h, k, c)

    def other(h):
        half = slice(h * 64, h * 64 + 64)
        for k in (0, 1, 2, 3):
            at("core", from_core, h, k)
            acc[half] += project(h, k, 1 - c)
        kvs[0, half] = acc[half, 128:256].astype(BF16)
        kvs[1, half] = acc[half, 256:384].astype(BF16)

    kv_copies = []
    for h in (0, 1):
        for i in (0, 1):
            kv_copies.append(
                pltpu.make_async_remote_copy(
                    src_ref=kvs.at[i, pl.ds(h * 64, 64)],
                    dst_ref=kvm.at[i, pl.ds(h * 64, 64)],
                    send_sem=kv_ss.at[h * 2 + i],
                    recv_sem=kv_rs.at[h * 2 + i],
                    device_id={"seq": nxt},
                    device_id_type=MESH,
                )
            )

    def pass_on(h):
        @pl.when(has_next & (turn != 1))
        def _():
            for copy in kv_copies[2 * h : 2 * h + 2]:
                copy.start()

    across(0)
    across(1)

    @pl.when(turn != 2)
    def _():
        share_weights()

    along(0, (0, 1, 2, 3))
    ld_wv.wait()
    same(0)
    along(1, (0, 1))
    other(0)

    @pl.when(turn != 2)
    def _():
        pl.semaphore_wait(ready, 1)
        doc_copy.start()

    pass_on(0)
    along(1, (2, 3))

    @pl.when(turn == 2)
    def _():
        share_weights()

    same(1)
    other(1)
    pass_on(1)

    ld_cb.wait()
    ld_pb.wait()
    query = acc[:, 0:128]
    qc = (query + cbias[...]).astype(BF16)
    qp = (query + pbias[...]).astype(BF16)
    pos = pltpu.roll(dot_t(qp, rel), 129, 1, stride=1, stride_axis=0)
    scale = F32(1.0) / jnp.sqrt(F32(128.0))
    own_doc = doc[...]
    row_doc = jnp.transpose(jnp.broadcast_to(own_doc, (128, 128)))
    rows = lax.broadcasted_iota(jnp.int32, (128, 128), 0)
    cols = lax.broadcasted_iota(jnp.int32, (128, 128), 1)
    ok_own = (cols <= rows) & (row_doc == own_doc)
    s_own = (dot_t(qc, kvs[0]) + pos[:, 128:256]) * scale
    s_own = jnp.where(ok_own, s_own, F32(-1e30))
    top_own = jnp.max(s_own, axis=1, keepdims=True)

    for h in (0, 1):
        sent(toks.at[h, pl.ds(0, sends[h])], tok_ss.at[h])
    with jax.named_scope("m_via"):
        relay_weights()

    @pl.when(has_prev)
    def _():
        doc_copy.wait_recv()

    @pl.when(seq == 0)
    def _():
        docm[...] = jnp.zeros_like(docm)
        kvm[...] = jnp.zeros_like(kvm)

    ok_mem = (row_doc == docm[...]) & (seq > 0)

    with jax.named_scope("m_kv0"):

        @pl.when(has_prev)
        def _():
            for copy in kv_copies[0:3]:
                copy.wait_recv()
    s_mem = (dot_t(qc, kvm[0]) + pos[:, 0:128]) * scale
    s_mem = jnp.where(ok_mem, s_mem, F32(-1e30))
    top = jnp.maximum(top_own, jnp.max(s_mem, axis=1, keepdims=True))
    e_own = jnp.where(ok_own, jnp.exp(s_own - top), F32(0.0))
    e_mem = jnp.where(ok_mem, jnp.exp(s_mem - top), F32(0.0))
    total = jnp.sum(e_own, axis=1, keepdims=True) + jnp.sum(e_mem, axis=1, keepdims=True)
    w_own = (e_own / total).astype(BF16)
    w_mem = (e_mem / total).astype(BF16)
    with jax.named_scope("m_kv1"):

        @pl.when(has_prev)
        def _():
            kv_copies[3].wait_recv()

    rows_in = 128 // BANDS
    for half in range(BANDS):
        band = slice(half * rows_in, half * rows_in + rows_in)
        head = dot(w_own[band], kvs[1]) + dot(w_mem[band], kvm[1])
        ho[half, xc] = head.astype(BF16)
        if half > 0:
            sent(ho.at[half - 1, pl.ds(0, 7)], ho_ss.at[half - 1])
        for n, (xx, cc) in enumerate(peers):
            copy = pltpu.make_async_remote_copy(
                src_ref=ho.at[half, xc],
                dst_ref=ho.at[half, xc],
                send_sem=ho_ss.at[half],
                recv_sem=ho_rs.at[half, n // 5],
                device_id={"mp": mp_of(z, xx, cc)},
                device_id_type=MESH,
            )
            copy.start()

    def term(half, xs, zz):
        slots = [xx * 2 + cc for xx in xs for cc in (0, 1)]
        left = jnp.concatenate([ho[half, j] for j in slots], axis=1)
        right = jnp.concatenate([wo[j, zz] for j in slots], axis=0)
        return dot(left, right)

    with jax.named_scope("m_wo"):
        pltpu.make_async_copy(wo.at[xc], wo.at[xc], lsem.at[3]).wait()
        arrived(wo.at[pl.ds(0, 7)], w_rs)

    @pl.when(turn == 1)
    def _():
        for copy in kv_copies:
            copy.start()

    for half in range(BANDS):
        with jax.named_scope(f"m_ho{half}"):
            arrived(ho.at[half, pl.ds(0, 5)], ho_rs.at[half, 0])
        for k in (3, 2, 1, 0):
            part[half, zo[k]] = term(half, (x, xr, xl), zo[k])
        with jax.named_scope(f"m_hof{half}"):
            arrived(ho.at[half, pl.ds(0, 2)], ho_rs.at[half, 1])
        for k in (3, 2, 1, 0):
            zz = zo[k]
            part[half, zz] += term(half, (x_far,), zz)
            if k > 0:
                copy = pltpu.make_async_remote_copy(
                    src_ref=part.at[half, zz],
                    dst_ref=rcv.at[half, z],
                    send_sem=p_ss.at[half],
                    recv_sem=p_rs.at[half],
                    device_id={"mp": mp_of(zz, x, c)},
                    device_id_type=MESH,
                )
                copy.start()

    sent(wst.at[pl.ds(0, 7)], w_ss)
    sent(via, via_ss)
    sent(ho.at[BANDS - 1, pl.ds(0, 7)], ho_ss.at[BANDS - 1])

    @pl.when(has_next)
    def _():
        for copy in kv_copies + [doc_copy]:
            copy.wait_send()

    for half in range(BANDS):
        with jax.named_scope(f"m_part{half}"):
            arrived(rcv.at[half, pl.ds(0, 3)], p_rs.at[half])
        result = part[half, z]
        for k in (1, 2, 3):
            result = result + rcv[half, zo[k]]
        out[half * rows_in : half * rows_in + rows_in, :] = result.astype(BF16)

    with jax.named_scope("m_send"):
        for half in range(BANDS):
            sent(part.at[half, pl.ds(0, 3)], p_ss.at[half])


def shards(tokens, w_qkv, w_pos, w_out, content_bias, position_bias, doc_ids):
    vmem = pl.BlockSpec(memory_space=pltpu.VMEM)
    hbm = pl.BlockSpec(memory_space=pltpu.HBM)
    sinus = jnp.asarray(sinus_reversed(256, 4096))
    operands = (
        tokens, w_qkv, w_pos, w_out, content_bias, position_bias, doc_ids.reshape(1, 128), sinus
    )
    operands = [pltpu.with_memory_space_constraint(a, pltpu.HBM) for a in operands]
    return pl.pallas_call(
        kernel,
        out_shape=pltpu.VMEM((128, 128), BF16),
        in_specs=[hbm] * 8,
        out_specs=vmem,
        scratch_shapes=[
            pltpu.VMEM((1, 128), F32),
            pltpu.VMEM((1, 128), F32),
            pltpu.VMEM((1, 128), jnp.int32),
            pltpu.VMEM((2, 32, 64, 128), BF16),
            pltpu.VMEM((3, 4096, 128), BF16),
            pltpu.VMEM((4096, 128), BF16),
            pltpu.VMEM((256, 4096), BF16),
            pltpu.VMEM((8, 4, 128, 128), BF16),
            pltpu.VMEM((128, 384), F32),
            pltpu.VMEM((2, 128, 128), BF16),
            pltpu.VMEM((2, 128, 128), BF16),
            pltpu.VMEM((1, 128), jnp.int32),
            pltpu.VMEM((BANDS, 8, 128 // BANDS, 128), BF16),
            pltpu.VMEM((BANDS, 4, 128 // BANDS, 128), F32),
            pltpu.VMEM((BANDS, 4, 128 // BANDS, 128), F32),
            pltpu.VMEM((8, 4, 128, 128), BF16),
            pltpu.VMEM((2, 4, 128, 128), BF16),
            pltpu.SemaphoreType.REGULAR,
            pltpu.SemaphoreType.DMA,
            pltpu.SemaphoreType.DMA((2,)),
            pltpu.SemaphoreType.DMA((11,)),
            pltpu.SemaphoreType.DMA((2,)),
            pltpu.SemaphoreType.DMA((2, 16)),
            pltpu.SemaphoreType.DMA((2, 4)),
            pltpu.SemaphoreType.DMA,
            pltpu.SemaphoreType.DMA,
            pltpu.SemaphoreType.DMA((5,)),
            pltpu.SemaphoreType.DMA((5,)),
            pltpu.SemaphoreType.DMA((BANDS,)),
            pltpu.SemaphoreType.DMA((BANDS, 2)),
            pltpu.SemaphoreType.DMA((BANDS,)),
            pltpu.SemaphoreType.DMA((BANDS,)),
        ],
        compiler_params=pltpu.CompilerParams(
            collective_id=0, has_side_effects=True, vmem_limit_bytes=20 * 1024 * 1024
        ),
        name="layer",
    )(*operands)


def solution(mesh):
    in_specs = (
        P("seq", "mp"),
        P(None, None, "mp"),
        P(None, "mp"),
        P("mp", None),
        P("mp", None),
        P("mp", None),
        P("seq"),
    )
    out_specs = P("seq", "mp")
    return jax.shard_map(shards, mesh=mesh, in_specs=in_specs, out_specs=out_specs, check_vma=False)
```

time: 47.9 us -> 46.5 us (0.971)
  Pallas kernels: 47.2 us -> 45.4 us
    pallas_call x1, Pallas kernels: 47.2 us -> 45.4 us  [shards(): pl.pallas_call(kernel, out_shape=pltpu.VMEM((128, 128), BF16), in_specs=[...]
where the time goes in v3:
time: 46.5 us; the launch traced here: 46 us
  Pallas kernels  45.4 us (98%)
  local copies, waits for them, and re-layouts  0.62 us (1%)
    pallas_call x1, Pallas kernels, shards(): pl.pallas_call(kernel, out_shape=pltpu.VMEM((128, 128), BF16), in_specs=[...  45.4 us

profile of v3, /device:TPU:56, one launch (start us, length us, event | category | flops | bytes accessed | tf_op | source)
XLA Modules:
  0.0 46.0 jit_solution(8083579732334993918)
XLA Ops:
  0.0 45.4 %layer.1 = bf16[128,128]{1,0:T(8,128)(2,1)S(1)} custom-call(bf16[128,128]{1,0:T(8,128)(2,1)} %tok_in.1, bf16[3,4096,128]{2,1,0:T(8,128)(2,1)} %wqkv.1, bf16[4096,128]{1,0:T(8,128)(2,1)} %wpos.1, bf16[128,4096]{1,0:T(8,128)(2,1)} %wout.1, f32[1,128]{1,0:T(1,128)} %cbias_in.1, f32[1,128]{1,0:T(1,128)} %pbias_in.1, s32[1,128]{1,0:T(1,128)} %bitcast.1, ...), custom_call_target="tpu_custom_call" | custom-call | tf_op jit(solution)/shard_map/layer/pallas_call | solution.py:481
  45.4 0.6 %copy.10 = bf16[128,128]{1,0:T(8,128)(2,1)} copy(bf16[128,128]{1,0:T(8,128)(2,1)S(1)} %layer.1) | data formatting | bytes 65536

commit v4 on v3

--- a/solution.py
+++ b/solution.py
@@ -308,7 +308,7 @@
             )
 
     def pass_on(h):
-        @pl.when(has_next & (turn != 1))
+        @pl.when(has_next & ((turn != 1) | (h == 0)))
         def _():
             for copy in kv_copies[2 * h : 2 * h + 2]:
                 copy.start()
@@ -424,7 +424,7 @@
 
     @pl.when(turn == 1)
     def _():
-        for copy in kv_copies:
+        for copy in kv_copies[2:4]:
             copy.start()
 
     for half in range(BANDS):

time: 46.5 us -> 46.6 us (level)
  no operation moved by 1% of the time
where the time goes in v4:
time: 46.6 us; the launch traced here: 46.4 us
  Pallas kernels  45.8 us (98%)
  local copies, waits for them, and re-layouts  0.62 us (1%)
    pallas_call x1, Pallas kernels, shards(): pl.pallas_call(kernel, out_shape=pltpu.VMEM((128, 128), BF16), in_specs=[...  45.8 us

profile of v4, /device:TPU:56, one launch (start us, length us, event | category | flops | bytes accessed | tf_op | source)
XLA Modules:
  0.0 46.4 jit_solution(18039162041801388650)
XLA Ops:
  0.0 45.8 %layer.1 = bf16[128,128]{1,0:T(8,128)(2,1)S(1)} custom-call(bf16[128,128]{1,0:T(8,128)(2,1)} %tok_in.1, bf16[3,4096,128]{2,1,0:T(8,128)(2,1)} %wqkv.1, bf16[4096,128]{1,0:T(8,128)(2,1)} %wpos.1, bf16[128,4096]{1,0:T(8,128)(2,1)} %wout.1, f32[1,128]{1,0:T(1,128)} %cbias_in.1, f32[1,128]{1,0:T(1,128)} %pbias_in.1, s32[1,128]{1,0:T(1,128)} %bitcast.1, ...), custom_call_target="tpu_custom_call" | custom-call | tf_op jit(solution)/shard_map/layer/pallas_call | solution.py:481
  45.8 0.6 %copy.10 = bf16[128,128]{1,0:T(8,128)(2,1)} copy(bf16[128,128]{1,0:T(8,128)(2,1)S(1)} %layer.1) | data formatting | bytes 65536
